TPU v7x, 256 devices: a whole 4x4x8 slice. The times are simulated.
256 devices in a mesh: dp: 32 (over x, y, core), ctx: 8 (over z).
Axes of the slice: x: 4, y: 4, z: 8, core: 2. Of those that a mesh axis runs over, the one named last changes fastest.
Arguments:
- cotangent: bfloat16 [32, 4096, 8192], P('dp', 'ctx'), may hold values from -6 to 6
- out_weight: bfloat16 [256, 8192], P(None, 'ctx'), may hold values from -0.0625 to 0.0625
- head_input: bfloat16 [32, 4096, 256], P('dp', 'ctx'), may hold values from -6 to 6
- injector: bfloat16 [32, 4096, 128], P('dp', 'ctx'), may hold values from -0.59765625 to 0.59765625
- readout: bfloat16 [32, 4096, 128], P('dp', 'ctx'), may hold values from -0.59765625 to 0.59765625
- decay_code: int32 [32, 4096, 2], P('dp', 'ctx'), may hold values from 1 to 40960
- decay_rate: float32 [2], replicated, may hold values from 4.8828125e-06 to 0.0061035156
- start_state: float32 [32, 8, 2, 128, 128], P('dp', 'ctx'), may hold values from -6 to 6
Outputs:
- gradient_input: bfloat16 [32, 4096, 256], P('dp', 'ctx')
- gradient_injector: float32 [32, 4096, 128], P('dp', 'ctx')
- gradient_readout: float32 [32, 4096, 128], P('dp', 'ctx')
- gradient_weight: float32 [256, 8192], P('ctx', 'dp')
- gradient_rate: float32 [2], replicated
All inputs are finite; a program needn't handle non-finite values.
Results may differ from a plain program's by a relative error of at most 0.0049.
Values may be sent and summed in bfloat16 or wider, within the bound.
No kernel may reach another device: no remote copies, remote signals or barrier semaphores. Data moves between devices by JAX's collectives and lax.ppermute only.
A program may use at most 128 MiB of HBM per device.

v0:
```python
import jax
import jax.numpy as jnp
from jax import lax
from jax.sharding import PartitionSpec as P

precise = lax.Precision.HIGHEST


def carried_in(value, axis, join, neutral):
    count, mine = (lax.axis_size(axis), lax.axis_index(axis))
    pieces = jax.tree.map(lambda part: lax.all_gather(part, axis), value)
    pieces = jax.tree.map(lambda part: part[::-1], pieces)
    mine = count - 1 - mine
    total = jax.tree.map(
        lambda part, zero: jnp.full_like(part, 0) + jnp.asarray(zero, part.dtype), value, neutral
    )

    def lap(position, total):
        longer = join(total, jax.tree.map(lambda part: part[position], pieces))
        return jax.tree.map(lambda new, old: jnp.where(position < mine, new, old), longer, total)

    return lax.fori_loop(0, count - 1, lap, total)


def decay_table(log_decay):
    cumulative = jnp.cumsum(log_decay, axis=0)
    length = log_decay.shape[0]
    row_index = lax.broadcasted_iota(jnp.int32, (length, length), 0)
    col_index = lax.broadcasted_iota(jnp.int32, (length, length), 1)
    causal = (row_index >= col_index)[None]
    spread = cumulative.T[:, :, None] - cumulative.T[:, None, :]
    weights = jnp.where(causal, jnp.exp(jnp.where(causal, spread, 0.0)), 0.0)
    return (cumulative, weights)


def forward_shard(head_input, injector, readout, log_decay, start_state):
    length, heads_count = log_decay.shape
    cumulative, weights = decay_table(log_decay)
    intersection = jnp.dot(readout, injector.T, preferred_element_type=jnp.float32)
    mixing = intersection[None] * weights
    inputs_heads = head_input.reshape(length, heads_count, -1).astype(jnp.float32)
    within = jnp.einsum("hts,shp->thp", mixing, inputs_heads, precision=precise)
    carried = jnp.einsum("tn,hpn->thp", readout.astype(jnp.float32), start_state, precision=precise)
    outputs = within + jnp.exp(cumulative)[:, :, None] * carried
    return outputs.reshape(length, -1).astype(jnp.bfloat16)


def chain_piece(readout, output_grad, log_decay):
    length, heads_count = log_decay.shape
    cumulative = jnp.cumsum(log_decay, axis=0)
    grad_heads = output_grad.reshape(length, heads_count, -1).astype(jnp.float32)
    scaled = jnp.exp(cumulative)[:, :, None] * readout.astype(jnp.float32)[:, None, :]
    adjoint = jnp.einsum("thp,thn->hpn", grad_heads, scaled, precision=precise)
    return (jnp.exp(cumulative[-1]), adjoint)


def backward_shard(head_input, injector, readout, output_grad, log_decay, start_state, incoming):
    length, heads_count = log_decay.shape
    cumulative, weights = decay_table(log_decay)
    inputs_narrow = head_input.reshape(length, heads_count, -1)
    grad_narrow = output_grad.reshape(length, heads_count, -1)
    inputs_heads = inputs_narrow.astype(jnp.float32)
    grad_heads = grad_narrow.astype(jnp.float32)
    inject_float = injector.astype(jnp.float32)
    read_float = readout.astype(jnp.float32)
    intersection = jnp.dot(readout, injector.T, preferred_element_type=jnp.float32)
    mixing = intersection[None] * weights
    to_end = jnp.exp(cumulative[-1][None, :] - cumulative)
    from_start = jnp.exp(cumulative)
    entering = jnp.einsum("sn,hpn->shp", inject_float, incoming, precision=precise)
    grad_input = (
        jnp.einsum("hts,thp->shp", mixing, grad_heads, precision=precise)
        + to_end[:, :, None] * entering
    )
    pairing = (
        jnp.einsum("thp,shp->hts", grad_narrow, inputs_narrow, preferred_element_type=jnp.float32)
        * weights
    )
    through_start = jnp.einsum("thp,hpn->thn", grad_heads, start_state, precision=precise)
    grad_read = jnp.einsum("hts,sn->tn", pairing, inject_float, precision=precise)
    grad_read = grad_read + jnp.einsum("th,thn->tn", from_start, through_start, precision=precise)
    input_state = jnp.einsum("shp,hpn->shn", inputs_heads, incoming, precision=precise)
    grad_inject = jnp.einsum("hts,tn->sn", pairing, read_float, precision=precise)
    grad_inject = grad_inject + jnp.einsum("sh,shn->sn", to_end, input_state, precision=precise)
    products = intersection[None] * pairing
    carried = (
        jnp.einsum("tn,hpn->thp", read_float, start_state, precision=precise)
        * from_start[:, :, None]
    )
    reaching = to_end * jnp.einsum("shn,sn->sh", input_state, inject_float, precision=precise)
    end_term = from_start[-1] * jnp.einsum(
        "hpn,hpn->h", incoming, start_state, precision=precise
    ) + jnp.sum(reaching, axis=0)
    cumul_grad = jnp.sum(products, axis=2).T - jnp.sum(products, axis=1).T
    cumul_grad = cumul_grad + jnp.sum(grad_heads * carried, axis=2) - reaching
    is_last = lax.broadcasted_iota(jnp.int32, (length, 1), 0) == length - 1
    cumul_grad = cumul_grad + jnp.where(is_last, end_term[None, :], 0.0)
    decay_grad = jnp.flip(jnp.cumsum(jnp.flip(cumul_grad, 0), axis=0), 0)
    rate_terms = jnp.sum(decay_grad * log_decay, axis=0)
    return (grad_input.reshape(length, -1).astype(jnp.bfloat16), grad_inject, grad_read, rate_terms)


def combine(earlier, later):
    return (later[0] * earlier[0], later[1] + later[0][:, None, None] * earlier[1])


def local(
    cotangent, out_weight, head_input, injector, readout, decay_code, decay_rate, start_state
):
    grad_out = cotangent[0]
    inputs_local = head_input[0]
    inject_local = injector[0]
    read_local = readout[0]
    state_local = start_state[0, 0]
    length = grad_out.shape[0]
    output_grad = lax.dot_general(
        grad_out,
        lax.all_gather(out_weight, "ctx", axis=1, tiled=True),
        (((1,), (1,)), ((), ())),
        preferred_element_type=jnp.float32,
    ).astype(jnp.bfloat16)
    log_decay = -decay_rate[None, :] * decay_code[0].astype(jnp.float32)
    decay_total, adjoint = chain_piece(read_local, output_grad, log_decay)
    identity = (jnp.ones_like(decay_total), jnp.zeros_like(adjoint))
    incoming = carried_in((decay_total, adjoint), "ctx", combine, identity)[1]
    outputs = forward_shard(inputs_local, inject_local, read_local, log_decay, state_local)
    local_weight = lax.dot_general(
        outputs, grad_out, (((0,), (0,)), ((), ())), preferred_element_type=jnp.float32
    )
    data_part = lax.psum_scatter(local_weight, "dp", scatter_dimension=1, tiled=True)
    weight_part = lax.psum_scatter(data_part, "ctx", scatter_dimension=0, tiled=True)
    grad_input, grad_inject, grad_read, rate_terms = backward_shard(
        inputs_local, inject_local, read_local, output_grad, log_decay, state_local, incoming
    )
    tokens_all = length * lax.axis_size("dp") * lax.axis_size("ctx")
    rate_sum = lax.psum(rate_terms, ("dp", "ctx"))
    return (
        grad_input[None],
        grad_inject[None],
        grad_read[None],
        weight_part,
        rate_sum / tokens_all,
    )


def solution(mesh):
    in_specs = (
        P("dp", "ctx", None),
        P(None, "ctx"),
        P("dp", "ctx", None),
        P("dp", "ctx", None),
        P("dp", "ctx", None),
        P("dp", "ctx", None),
        P(),
        P("dp", "ctx", None, None, None),
    )
    out_specs = (
        P("dp", "ctx", None),
        P("dp", "ctx", None),
        P("dp", "ctx", None),
        P("ctx", "dp"),
        P(),
    )
    return jax.shard_map(local, mesh=mesh, in_specs=in_specs, out_specs=out_specs, check_vma=False)
```

profile of v0, /device:TPU:2, one launch (start us, length us, event | category | flops | bytes accessed | tf_op | source)
XLA Modules:
  0.0 262.4 jit_solution(3269358175071123547)
XLA Ops:
  7.2 0.7 all-gather.5.cloned.1.call-update
  7.9 0.0 all-gather.7.cloned.1.call-start
  7.9 0.7 neg.4
  8.6 0.8 fusion.61
  9.4 0.6 reduce-window.14
  10.0 0.2 slice_reduce_fusion.1
  10.1 0.2 reduce-window.15
  10.3 0.9 bitcast_convert_fusion.1
  11.3 0.1 copy.52
  11.4 0.1 add_bitcast_fusion.1
  11.5 56.1 %all-gather.5.cloned.1.call-done = bf16[256,8192]{1,0:T(8,128)(2,1)} async-done(((bf16[256,1024]{1,0:T(8,128)(2,1)}), bf16[256,8192]{1,0:T(8,128)(2,1)}) %all-gather.5.cloned.1.call-update) | async-done | bytes 4194320 | tf_op jit(solution)/shard_map/all_gather | solution.py:118
  67.6 6.9 %fusion.26 = bf16[512,256]{0,1:T(8,128)(2,1)S(1)} fusion(bf16[256,8192]{1,0:T(8,128)(2,1)} %all-gather.5.cloned.1.call-done, bf16[1,512,8192]{2,1,0:T(8,128)(2,1)} %param.10), kind=kOutput, calls=%fused_computation.24 | convolution fusion | flops 2147614720 | bytes 12845056 | tf_op jit(solution)/shard_map/dot_general | solution.py:116
  74.6 1.1 fusion.43
  75.7 0.0 reduce-scatter.3.cloned.1.call-start
  75.7 0.1 copy.91
  75.9 0.1 iota_compare_fusion
  76.0 0.3 fusion.55
  76.3 0.4 multiply_reduce_fusion.2
  76.8 2.0 fusion.22
  78.7 9.1 %fusion.1 = f32[256,8192]{1,0:T(8,128)} fusion(bf16[512,256]{0,1:T(8,128)(2,1)S(1)} %bitcast.164, bf16[1,512,8192]{2,1,0:T(8,128)(2,1)} %param.10), kind=kOutput, calls=%fused_computation.3 | convolution fusion | flops 2147483648 | bytes 17039360 | tf_op jit(solution)/shard_map/dot_general | solution.py:127
  87.8 0.0 reduce-scatter.5.cloned.1.call-start
  87.9 0.2 slice_reduce_fusion.3
  88.0 14.7 %all-gather.1 = f32[8,1,2]{2,1,0:T(1,128)S(1)} all-gather(f32[1,1,2]{2,1,0:T(1,128)S(1)} %bitcast.175), channel_id=1, replica_groups=mesh['dp'=32,'ctx'=8] {'ctx'}, dimensions={0}, use_global_device_ids=true | all-gather | bytes 72 | tf_op jit(solution)/shard_map/all_gather | solution.py:11
  102.8 0.1 copy.54
  102.9 0.1 rev.14
  103.0 0.1 copy.55
  103.0 0.1 copy.72
  103.2 0.1 copy.89
  103.4 0.2 slice_reduce_fusion.2
  103.6 0.4 convolution_bitcast_fusion
  104.0 4.4 %fusion.45 = f32[512,1,128]{2,1,0:T(1,128)} fusion(f32[512,2,1]{1,2,0:T(1,128)S(1)} %copy.72, f32[512,2,128]{2,0,1:T(8,128)S(1)} %convolution_bitcast_fusion), kind=kOutput, calls=%fused_computation.47 | convolution fusion | flops 1572864 | bytes 790528 | tf_op jit(solution)/shard_map/th,thn->tn/dot_general | solution.py:81
  108.4 2.4 fusion.11
  110.8 2.2 multiply_reduce_fusion
  113.0 0.1 all-gather.7.cloned.1.call-done
  113.1 1.3 rev.13
  114.5 0.9 while.14
  114.5 0.1 fusion.81
  114.6 0.1 fusion.81
  114.8 0.1 fusion.81
  114.9 0.1 fusion.81
  115.0 0.1 fusion.81
  115.2 0.1 fusion.81
  115.3 0.1 fusion.81
  115.4 0.1 fusion.49
  115.5 0.4 fusion.41
  115.9 0.2 multiply_reduce_fusion.4
  116.1 0.1 fusion.60
  116.2 0.4 rev.15
  116.6 0.6 reduce-window.16
  117.2 0.2 slice_reduce_fusion
  117.4 0.2 reduce-window.19
  117.5 0.1 add_bitcast_fusion
  117.6 0.4 rev.16
  118.0 0.2 multiply_reduce_fusion.3
  118.2 1.3 fusion.29
  119.5 75.2 %psum.7 = f32[2]{0:T(128)S(1)} all-reduce(f32[2]{0:T(128)S(1)} %multiply_reduce_fusion.3), channel_id=1, replica_groups=mesh['dp'=32,'ctx'=8] {'dp','ctx'}, use_global_device_ids=true, to_apply=%region_14.15 | all-reduce | flops 2 | bytes 16 | tf_op jit(solution)/shard_map/psum | solution.py:136
  194.7 0.1 fusion.42
  194.8 0.1 copy.70
  194.9 21.4 %reduce-scatter.3.cloned.1.call-done = f32[256,256]{1,0:T(8,128)} async-done(((f32[256,8192]{1,0:T(8,128)}), f32[256,256]{1,0:T(8,128)}) %reduce-scatter.3.cloned.1.call-update) | async-done | bytes 262160 | tf_op jit(solution)/shard_map/reduce_scatter | solution.py:130
  216.3 0.4 fusion.25
  216.7 0.8 copy.62
  217.6 1.7 fusion.30
  219.3 0.5 broadcast_multiply_fusion
  219.8 36.1 %reduce-scatter.5.cloned.1.call-done = f32[32,256]{1,0:T(8,128)} async-done(((f32[256,256]{1,0:T(8,128)}), f32[32,256]{1,0:T(8,128)}) %reduce-scatter.5.cloned.1.call-update) | async-done | bytes 32784 | tf_op jit(solution)/shard_map/reduce_scatter | solution.py:131
  (36 shorter events, 0.3 us)
Async XLA Ops:
  7.2 60.4 %all-gather.5.cloned.1.call-start = ((), (), s32[]{:S(2)}) async-start(), calls=%async_computation.2 | async-start | bytes 4718592 | tf_op jit(solution)/shard_map/all_gather | solution.py:118
  7.9 105.2 %all-gather.7.cloned.1.call-start = ((), (), s32[]{:S(2)}) async-start(), calls=%async_computation.5 | async-start | bytes 1179648 | tf_op jit(solution)/shard_map/all_gather | solution.py:11
  11.5 64.2 %copy-start.4 = (bf16[1,512,256]{2,1,0:T(8,128)(2,1)S(1)}, bf16[1,512,256]{2,1,0:T(8,128)(2,1)}, u32[]{:S(2)}) copy-start(bf16[1,512,256]{2,1,0:T(8,128)(2,1)} %param.12) | copy-start | bytes 786436
  11.5 64.5 %copy-start = (bf16[1,512,128]{2,1,0:T(8,128)(2,1)S(1)}, bf16[1,512,128]{2,1,0:T(8,128)(2,1)}, u32[]{:S(2)}) copy-start(bf16[1,512,128]{2,1,0:T(8,128)(2,1)} %param.13) | copy-start | bytes 393220
  11.5 64.5 %copy-start.1 = (bf16[1,512,128]{2,1,0:T(8,128)(2,1)S(1)}, bf16[1,512,128]{2,1,0:T(8,128)(2,1)}, u32[]{:S(2)}) copy-start(bf16[1,512,128]{2,1,0:T(8,128)(2,1)} %param.14) | copy-start | bytes 393220
  74.5 1.8 copy-start.2
  75.7 140.6 %reduce-scatter.3.cloned.1.call-start = ((), (), s32[]{:S(2)}) async-start(), calls=%async_computation.3 | async-start | bytes 8650752 | tf_op jit(solution)/shard_map/reduce_scatter | solution.py:130
  76.0 32.4 %copy-start.5 = (pred[512,512]{1,0:T(8,128)(4,1)}, pred[512,512]{1,0:T(8,128)(4,1)S(1)}, u32[]{:S(2)}) copy-start(pred[512,512]{1,0:T(8,128)(4,1)S(1)} %iota_compare_fusion) | copy-start | bytes 786436
  87.8 168.0 %reduce-scatter.5.cloned.1.call-start = ((), (), s32[]{:S(2)}) async-start(), calls=%async_computation.4 | async-start | bytes 294912 | tf_op jit(solution)/shard_map/reduce_scatter | solution.py:131
  114.4 3.5 %copy-start.7 = (s32[1,512,2]{1,2,0:T(2,128)S(1)}, s32[1,512,2]{1,2,0:T(2,128)}, u32[]{:S(2)}) copy-start(s32[1,512,2]{1,2,0:T(2,128)} %param.15) | copy-start | bytes 12292
  114.5 3.7 %copy-start.6 = (f32[512,1,128]{2,1,0:T(1,128)S(1)}, f32[512,1,128]{2,1,0:T(1,128)}, u32[]{:S(2)}) copy-start(f32[512,1,128]{2,1,0:T(1,128)} %fusion.45) | copy-start | bytes 786436
  115.5 100.8 %copy-start.3 = (f32[512,2,128]{0,2,1:T(8,128)S(1)}, f32[512,2,128]{0,2,1:T(8,128)}, u32[]{:S(2)}) copy-start(f32[512,2,128]{0,2,1:T(8,128)} %fusion.11) | copy-start | bytes 1572868
Sparse Core Ops, SparseCore 0:
  9.8 57.7 all-gather.4
  75.8 37.3 all-gather.6
  117.2 99.0 reduce-scatter.2
  219.4 36.4 reduce-scatter.4
where the time goes:
time: 263 us; the launch traced here: 262 us
  waiting for transfers between devices  114 us (43%)
  blocking collectives  89.9 us (34%)
  matrix products  33.1 us (13%)
  between operations  14 us (5%)
  other arithmetic  5.93 us (2%)
  local copies, waits for them, and re-layouts  4.61 us (2%)
    psum x1, blocking collectives, local(): rate_sum = lax.psum(rate_terms, ('dp', 'ctx'))  75.2 us
    all_gather x1, waiting for transfers between devices, local(): lax.all_gather(out_weight, 'ctx', axis=1, tiled=True)  56.1 us
    reduce_scatter x1, waiting for transfers between devices, local(): lax.psum_scatter(data_part, 'ctx', scatter_dimension=0, tiled=True)  36.1 us
    reduce_scatter x1, waiting for transfers between devices, local(): lax.psum_scatter(local_weight, 'dp', scatter_dimension=1, tiled=True)  21.4 us
    all_gather x1, blocking collectives, carried_in(): pieces = jax.tree.map(lambda part: lax.all_gather(part, axis), value)  14.7 us
    dot_general x1, matrix products, local(): lax.dot_general(outputs, grad_out, (((0,), (0,)), ((), ())), preferred_el...  9.06 us
    dot_general x1, matrix products, local(): lax.dot_general(grad_out, lax.all_gather(out_weight, 'ctx', axis=1, tiled...  6.93 us
  transfers between devices with their start and end apart: 4, of which 4 were waited for; matrix products, arithmetic and copies ran while one was open for 14% of the time, Pallas kernels for 0%

commit v1 on v0

--- a/solution.py
+++ b/solution.py
@@ -2,8 +2,15 @@
 import jax.numpy as jnp
 from jax import lax
 from jax.sharding import PartitionSpec as P
+from jax.lax import all_to_all, psum
 
 precise = lax.Precision.HIGHEST
+
+
+def ticks_assign(packet):
+    aux = jnp.concatenate([packet for _ in range(psum(1, "ctx"))], 1)
+    ready = all_to_all(aux, "ctx", 1, 1, tiled=True)
+    return ready
 
 
 def carried_in(value, axis, join, neutral):
@@ -115,7 +122,7 @@
     length = grad_out.shape[0]
     output_grad = lax.dot_general(
         grad_out,
-        lax.all_gather(out_weight, "ctx", axis=1, tiled=True),
+        ticks_assign(out_weight),
         (((1,), (1,)), ((), ())),
         preferred_element_type=jnp.float32,
     ).astype(jnp.bfloat16)

time: 263 us -> 296 us (1.13)
  local copies, waits for them, and re-layouts: 4.61 us -> 21 us
  waiting for transfers between devices: 114 us -> 123 us
  starting transfers between devices: 0.16 us -> 8.73 us
    all_to_all x0 -> x1, waiting for transfers between devices: none -> 95 us  [ticks_assign(): ready = all_to_all(aux, 'ctx', 1, 1, tiled=True)]
    all_gather x1 -> x0, waiting for transfers between devices: 56.1 us -> none  [local(): lax.all_gather(out_weight, 'ctx', axis=1, tiled=True)]
    reduce_scatter x1, waiting for transfers between devices: 21.4 us -> 0.03 us  [local(): lax.psum_scatter(local_weight, 'dp', scatter_dimension=1, tiled=True)]
    all_to_all x0 -> x2, local copies, waits for them, and re-layouts: none -> 12.9 us  [ticks_assign(): ready = all_to_all(aux, 'ctx', 1, 1, tiled=True)]
    all_to_all x0 -> x1, starting transfers between devices: none -> 8.6 us  [ticks_assign(): ready = all_to_all(aux, 'ctx', 1, 1, tiled=True)]
    reduce_scatter x1, waiting for transfers between devices: 36.1 us -> 28.4 us  [local(): lax.psum_scatter(data_part, 'ctx', scatter_dimension=0, tiled=True)]
    unnamed x21 -> x31, local copies, waits for them, and re-layouts: 1.11 us -> 4.51 us
  transfers between devices with their start and end apart: 4 -> 4, of which waited for: 4 -> 2; matrix products, arithmetic and copies ran while one was open for 14% -> 12% of each run, Pallas kernels for 0% -> 0%
where the time goes in v1:
time: 296 us; the launch traced here: 295 us
  waiting for transfers between devices  123 us (42%)
  blocking collectives  88 us (30%)
  matrix products  34.5 us (12%)
  local copies, waits for them, and re-layouts  21 us (7%)
  between operations  15.8 us (5%)
  starting transfers between devices  8.73 us (3%)
  other arithmetic  3.66 us (1%)
    all_to_all x1, waiting for transfers between devices, ticks_assign(): ready = all_to_all(aux, 'ctx', 1, 1, tiled=True)  95 us
    psum x1, blocking collectives, local(): rate_sum = lax.psum(rate_terms, ('dp', 'ctx'))  74.2 us
    reduce_scatter x1, waiting for transfers between devices, local(): lax.psum_scatter(data_part, 'ctx', scatter_dimension=0, tiled=True)  28.4 us
    all_gather x1, blocking collectives, carried_in(): pieces = jax.tree.map(lambda part: lax.all_gather(part, axis), value)  13.8 us
    all_to_all x2, local copies, waits for them, and re-layouts, ticks_assign(): ready = all_to_all(aux, 'ctx', 1, 1, tiled=True)  12.9 us
    dot_general x1, matrix products, local(): lax.dot_general(outputs, grad_out, (((0,), (0,)), ((), ())), preferred_el...  8.95 us
    all_to_all x1, starting transfers between devices, ticks_assign(): ready = all_to_all(aux, 'ctx', 1, 1, tiled=True)  8.6 us
    dot_general x1, matrix products, local(): lax.dot_general(grad_out, ticks_assign(out_weight), (((1,), (1,)), ((), (...  7.08 us
  transfers between devices with their start and end apart: 4, of which 2 were waited for; matrix products, arithmetic and copies ran while one was open for 12% of the time, Pallas kernels for 0%

profile of v1, /device:TPU:2, one launch (start us, length us, event | category | flops | bytes accessed | tf_op | source)
XLA Modules:
  0.0 295.5 jit_solution(9387877463644981656)
XLA Ops:
  8.0 1.2 copy.52
  9.6 1.9 copy-done
  11.5 6.5 %copy.60 = bf16[256,8,1024]{2,0,1:T(8,128)(2,1)} copy(bf16[256,8,1024]{0,2,1:T(8,128)(2,1)} %bitcast.159) | data formatting | bytes 8388608 | tf_op jit(solution)/shard_map/all_to_all | solution.py:12
  18.0 8.6 %all-to-all-start = ((bf16[256,8,1024]{2,0,1:T(8,128)(2,1)}), bf16[256,8,1024]{2,0,1:T(8,128)(2,1)}, u32[]{:S(2)}, u32[]{:S(2)}) async-start(bf16[256,8,1024]{2,0,1:T(8,128)(2,1)} %copy.60), calls=%async_computation | async-start | bytes 8388608 | tf_op jit(solution)/shard_map/all_to_all | solution.py:12
  26.6 0.0 all-gather.4.cloned.1.call-start
  26.7 0.1 fusion.61
  26.8 0.6 reduce-window.14
  27.4 0.2 slice_reduce_fusion.1
  27.5 0.2 reduce-window.15
  27.7 0.1 copy.62
  27.9 0.1 add_bitcast_fusion.1
  27.9 95.0 %all-to-all-done = bf16[256,8,1024]{2,0,1:T(8,128)(2,1)} async-done(((bf16[256,8,1024]{2,0,1:T(8,128)(2,1)}), bf16[256,8,1024]{2,0,1:T(8,128)(2,1)}, u32[]{:S(2)}, u32[]{:S(2)}) %all-to-all-start) | async-done | bytes 4194336 | tf_op jit(solution)/shard_map/all_to_all | solution.py:12
  123.0 6.4 %copy.61 = bf16[256,8,1024]{0,2,1:T(8,128)(2,1)} copy(bf16[256,8,1024]{2,0,1:T(8,128)(2,1)} %all-to-all-done) | data formatting | bytes 8388608 | tf_op jit(solution)/shard_map/all_to_all | solution.py:12
  129.4 7.1 %fusion.26 = bf16[256,512]{1,0:T(8,128)(2,1)S(1)} fusion(bf16[256,8192]{0,1:T(8,128)(2,1)} %bitcast.160, bf16[1,512,8192]{2,1,0:T(8,128)(2,1)} %param.10), kind=kOutput, calls=%fused_computation.24 | convolution fusion | flops 2147614720 | bytes 12845056 | tf_op jit(solution)/shard_map/dot_general | solution.py:123
  136.5 1.1 fusion.43
  137.6 0.0 reduce-scatter.3.cloned.1.call-start
  137.7 0.1 copy.101
  137.9 0.1 iota_compare_fusion
  137.9 0.3 fusion.55
  138.3 0.4 multiply_reduce_fusion.2
  138.7 2.0 fusion.22
  140.7 9.0 %fusion.1 = f32[256,8192]{1,0:T(8,128)} fusion(bf16[512,256]{0,1:T(8,128)(2,1)S(1)} %bitcast.170, bf16[1,512,8192]{2,1,0:T(8,128)(2,1)} %param.10), kind=kOutput, calls=%fused_computation.3 | convolution fusion | flops 2147483648 | bytes 17039360 | tf_op jit(solution)/shard_map/dot_general | solution.py:134
  149.7 0.0 reduce-scatter.5.cloned.1.call-start
  149.7 0.2 slice_reduce_fusion.3
  149.9 13.8 %all-gather.1 = f32[8,1,2]{2,1,0:T(1,128)S(1)} all-gather(f32[1,1,2]{2,1,0:T(1,128)S(1)} %bitcast.181), channel_id=1, replica_groups=mesh['dp'=32,'ctx'=8] {'ctx'}, dimensions={0}, use_global_device_ids=true | all-gather | bytes 72 | tf_op jit(solution)/shard_map/all_gather | solution.py:18
  163.7 0.1 copy.64
  163.8 0.1 rev.14
  163.9 0.1 copy.65
  164.0 0.1 copy.99
  164.1 0.1 copy.82
  164.3 0.2 slice_reduce_fusion.2
  164.5 0.4 convolution_bitcast_fusion
  164.9 4.4 %fusion.45 = f32[512,1,128]{2,1,0:T(1,128)} fusion(f32[512,2,1]{1,2,0:T(1,128)S(1)} %copy.82, f32[512,2,128]{2,0,1:T(8,128)S(1)} %convolution_bitcast_fusion), kind=kOutput, calls=%fused_computation.47 | convolution fusion | flops 1572864 | bytes 790528 | tf_op jit(solution)/shard_map/th,thn->tn/dot_general | solution.py:88
  169.3 2.4 fusion.11
  171.7 2.5 multiply_reduce_fusion
  174.3 1.4 rev.13
  175.7 0.9 while.14
  175.7 0.1 fusion.81
  175.9 0.1 fusion.81
  176.0 0.1 fusion.81
  176.1 0.1 fusion.81
  176.2 0.1 fusion.81
  176.4 0.1 fusion.81
  176.5 0.1 fusion.81
  176.6 0.1 fusion.49
  176.7 0.4 fusion.41
  177.1 0.2 multiply_reduce_fusion.4
  177.3 0.1 fusion.60
  177.4 0.4 rev.15
  177.8 0.6 reduce-window.16
  178.4 0.2 slice_reduce_fusion
  178.6 0.2 reduce-window.19
  178.7 0.1 add_bitcast_fusion
  178.8 0.4 rev.16
  179.2 0.2 multiply_reduce_fusion.3
  179.4 1.3 fusion.29
  180.7 74.2 %psum.7 = f32[2]{0:T(128)S(1)} all-reduce(f32[2]{0:T(128)S(1)} %multiply_reduce_fusion.3), channel_id=1, replica_groups=mesh['dp'=32,'ctx'=8] {'dp','ctx'}, use_global_device_ids=true, to_apply=%region_14.15 | all-reduce | flops 2 | bytes 16 | tf_op jit(solution)/shard_map/psum | solution.py:143
  254.9 0.1 fusion.42
  255.0 0.1 copy.80
  255.2 1.4 fusion.25
  256.6 0.8 copy.72
  257.5 1.7 fusion.30
  259.2 0.5 broadcast_multiply_fusion
  259.7 28.4 %reduce-scatter.5.cloned.1.call-done = f32[32,256]{1,0:T(8,128)} async-done(((f32[256,256]{1,0:T(8,128)}), f32[32,256]{1,0:T(8,128)}) %reduce-scatter.5.cloned.1.call-update) | async-done | bytes 32784 | tf_op jit(solution)/shard_map/reduce_scatter | solution.py:138
  (48 shorter events, 0.6 us)
Async XLA Ops:
  9.6 1.9 copy-start
  18.0 8.7 %copy-start.8 = (f32[2]{0:T(128)S(1)}, f32[2]{0:T(128)}, u32[]{:S(2)}) copy-start(f32[2]{0:T(128)} %param.16) | copy-start | bytes 28
  18.0 8.7 %copy-start.7 = (s32[1,512,2]{1,2,0:T(2,128)S(1)}, s32[1,512,2]{1,2,0:T(2,128)}, u32[]{:S(2)}) copy-start(s32[1,512,2]{1,2,0:T(2,128)} %param.15) | copy-start | bytes 12292
  18.0 9.7 %copy-start.2 = (bf16[1,512,128]{2,1,0:T(8,128)(2,1)S(1)}, bf16[1,512,128]{2,1,0:T(8,128)(2,1)}, u32[]{:S(2)}) copy-start(bf16[1,512,128]{2,1,0:T(8,128)(2,1)} %param.14) | copy-start | bytes 393220
  18.0 105.0 %all-to-all-start = ((bf16[256,8,1024]{2,0,1:T(8,128)(2,1)}), bf16[256,8,1024]{2,0,1:T(8,128)(2,1)}, u32[]{:S(2)}, u32[]{:S(2)}) async-start(bf16[256,8,1024]{2,0,1:T(8,128)(2,1)} %copy.60), calls=%async_computation | async-start | bytes 8388608 | tf_op jit(solution)/shard_map/all_to_all | solution.py:12
  26.6 147.7 %all-gather.4.cloned.1.call-start = ((), (), s32[]{:S(2)}) async-start(), calls=%async_computation.5 | async-start | bytes 1179648 | tf_op jit(solution)/shard_map/all_gather | solution.py:18
  129.4 8.3 %copy-start.5 = (bf16[1,512,256]{2,1,0:T(8,128)(2,1)S(1)}, bf16[1,512,256]{2,1,0:T(8,128)(2,1)}, u32[]{:S(2)}) copy-start(bf16[1,512,256]{2,1,0:T(8,128)(2,1)} %param.12) | copy-start | bytes 786436
  129.4 8.5 %copy-start.1 = (bf16[1,512,128]{2,1,0:T(8,128)(2,1)S(1)}, bf16[1,512,128]{2,1,0:T(8,128)(2,1)}, u32[]{:S(2)}) copy-start(bf16[1,512,128]{2,1,0:T(8,128)(2,1)} %param.13) | copy-start | bytes 393220
  129.4 8.8 %copy-start.3 = (f32[1,1,2,128,128]{4,3,2,1,0:T(8,128)S(1)}, f32[1,1,2,128,128]{4,3,2,1,0:T(8,128)}, u32[]{:S(2)}) copy-start(f32[1,1,2,128,128]{4,3,2,1,0:T(8,128)} %param.17) | copy-start | bytes 393220
  137.6 117.5 %reduce-scatter.3.cloned.1.call-start = ((), (), s32[]{:S(2)}) async-start(), calls=%async_computation.3 | async-start | bytes 8650752 | tf_op jit(solution)/shard_map/reduce_scatter | solution.py:137
  138.3 31.1 %copy-start.4 = (f32[512,512]{1,0:T(8,128)}, f32[512,512]{1,0:T(8,128)S(1)}, u32[]{:S(2)}) copy-start(f32[512,512]{1,0:T(8,128)S(1)} %fusion.55) | copy-start | bytes 3145732
  149.7 138.4 %reduce-scatter.5.cloned.1.call-start = ((), (), s32[]{:S(2)}) async-start(), calls=%async_computation.4 | async-start | bytes 294912 | tf_op jit(solution)/shard_map/reduce_scatter | solution.py:138
  174.3 5.1 %copy-start.6 = (f32[512,1,128]{2,1,0:T(1,128)S(1)}, f32[512,1,128]{2,1,0:T(1,128)}, u32[]{:S(2)}) copy-start(f32[512,1,128]{2,1,0:T(1,128)} %fusion.45) | copy-start | bytes 786436
Sparse Core Ops, SparseCore 0:
  137.8 34.8 all-gather.3
  255.3 32.6 reduce-scatter.4
Sparse Core Ops, SparseCore 1:
  149.7 96.3 reduce-scatter.2
